TPU v7x, 32 devices: a whole 2x2x4 slice. The times are simulated.
32 devices in a mesh: fsdp: 32 (over z, y, x, core).
Axes of the slice: x: 2, y: 2, z: 4, core: 2. Of those that a mesh axis runs over, the one named last changes fastest.
Arguments:
- hidden: bfloat16 [2, 32, 128, 1024], P(None, 'fsdp'), may hold values from -6 to 6
- encoder: bfloat16 [2, 32, 256, 1024], P(None, 'fsdp'), may hold values from -6 to 6
- cotangent: bfloat16 [2, 32, 128, 1024], P(None, 'fsdp'), may hold values from -6 to 6
- segment_ids: int32 [2, 32, 128], replicated, may hold values from 0 to 3, never falling along the last dimension, each value on 1 to 64 neighbouring positions
- rel_buckets: int32 [2, 32, 128], replicated, may hold values from 0 to 31
- enc_rows: int32 [2, 32], replicated, may hold values from 64 to 256, as said below
- dealing: int32 [2, 32], replicated, may hold values from 0 to 31, each once within a row
- gain_self: bfloat16 [1024], P('fsdp'), may hold values from 0.5 to 1.5
- gain_cross: bfloat16 [1024], P('fsdp'), may hold values from 0.5 to 1.5
- gain_ffn: bfloat16 [1024], P('fsdp'), may hold values from 0.5 to 1.5
- rel_bias: bfloat16 [512], P('fsdp'), may hold values from -4 to 4
- self_query: bfloat16 [1024, 1024], P('fsdp'), may hold values from -0.046875 to 0.046875
- self_key: bfloat16 [1024, 1024], P('fsdp'), may hold values from -0.1875 to 0.1875
- self_value: bfloat16 [1024, 1024], P('fsdp'), may hold values from -0.1875 to 0.1875
- self_out: bfloat16 [1024, 1024], P('fsdp'), may hold values from -0.5 to 0.5
- cross_query: bfloat16 [1024, 1024], P('fsdp'), may hold values from -0.046875 to 0.046875
- cross_key: bfloat16 [1024, 1024], P('fsdp'), may hold values from -0.1875 to 0.1875
- cross_value: bfloat16 [1024, 1024], P('fsdp'), may hold values from -0.1875 to 0.1875
- cross_out: bfloat16 [1024, 1024], P('fsdp'), may hold values from -0.5 to 0.5
- feed_gate: bfloat16 [1024, 2816], P('fsdp'), may hold values from -0.1875 to 0.1875
- feed_up: bfloat16 [1024, 2816], P('fsdp'), may hold values from -0.1875 to 0.1875
- feed_down: bfloat16 [2816, 1024], P('fsdp'), may hold values from -0.15625 to 0.15625
Outputs:
- layer_out: bfloat16 [2, 32, 128, 1024], P(None, 'fsdp')
- grad_hidden: float32 [2, 32, 128, 1024], P(None, 'fsdp')
- grad_encoder: float32 [2, 32, 256, 1024], P(None, 'fsdp')
- grad_gain_self: float32 [1024], P('fsdp')
- grad_gain_cross: float32 [1024], P('fsdp')
- grad_gain_ffn: float32 [1024], P('fsdp')
- grad_rel_bias: float32 [512], P('fsdp')
- grad_self_query: float32 [1024, 1024], P('fsdp')
- grad_self_key: float32 [1024, 1024], P('fsdp')
- grad_self_value: float32 [1024, 1024], P('fsdp')
- grad_self_out: float32 [1024, 1024], P('fsdp')
- grad_cross_query: float32 [1024, 1024], P('fsdp')
- grad_cross_key: float32 [1024, 1024], P('fsdp')
- grad_cross_value: float32 [1024, 1024], P('fsdp')
- grad_cross_out: float32 [1024, 1024], P('fsdp')
- grad_feed_gate: float32 [1024, 2816], P('fsdp')
- grad_feed_up: float32 [1024, 2816], P('fsdp')
- grad_feed_down: float32 [2816, 1024], P('fsdp')
Inputs may be any that keep to these rules, and one draw needn't show every extreme that they name: `enc_rows`: live encoder rows of each block; in every micro-batch some block has all 256. `dealing`: each micro-batch's row names every block once. `segment_ids`: document ids never fall along a block; a document has at most 64 tokens.
All inputs are finite; a program needn't handle non-finite values.
Results may differ from a plain program's by a relative error of at most 0.02.
The roundings to bfloat16 on the way count: a program that leaves them out, or rounds other values in their place, can miss the bound.
Values may be sent and summed in bfloat16 or wider, within the bound.
A program may use at most 192 MiB of HBM per device.

v0:
```python
import jax
import jax.numpy as jnp
from jax import lax
from jax.sharding import PartitionSpec as P

D = 1024
H = 16
DH = 64
NB = 32


eps_norm = 1e-06
masked_score = -1000000000.0
highest = lax.Precision.HIGHEST


def product(left_side, right_side):
    return jnp.dot(left_side, right_side, preferred_element_type=jnp.float32)


def product_left(left_side, right_side):
    return lax.dot_general(
        left_side, right_side, (((0,), (0,)), ((), ())), preferred_element_type=jnp.float32
    )


def product_right(left_side, right_side):
    return lax.dot_general(
        left_side, right_side, (((1,), (1,)), ((), ())), preferred_element_type=jnp.float32
    )


def scaled_norm(values, gain_row):
    mean_square = jnp.mean(values * values, axis=-1, keepdims=True)
    return values * lax.rsqrt(mean_square + eps_norm) * gain_row.astype(jnp.float32)


def gated_gelu(gate_pre, upward):
    return jax.nn.gelu(gate_pre, approximate=True) * upward


def head_split(matrix):
    return matrix.reshape(matrix.shape[0], H, DH)


def toeplitz_expand(per_offset):
    head_count, length = per_offset.shape
    filler = jnp.zeros((head_count, 1), jnp.float32)
    pattern = jnp.concatenate(
        [per_offset[:, :1], filler, per_offset[:, ::-1][:, : length - 1]], axis=1
    )
    tiled_rows = jnp.broadcast_to(pattern[:, None, :], (head_count, length, length + 1))
    return tiled_rows.reshape(head_count, length * (length + 1))[:, : length * length].reshape(
        head_count, length, length
    )


def toeplitz_fold(score_grid):
    head_count, length = (score_grid.shape[0], score_grid.shape[1])
    flat_grid = score_grid.reshape(head_count, length * length)
    padded = jnp.concatenate([flat_grid, jnp.zeros((head_count, length), jnp.float32)], axis=1)
    columns = jnp.sum(padded.reshape(head_count, length, length + 1), axis=1)
    return jnp.concatenate([columns[:, :1], columns[:, 2:][:, ::-1]], axis=1)


def score_block(queries, keys_in, bias_grid, allowed):
    scores = (
        jnp.einsum(
            "ihd,jhd->hij",
            head_split(queries),
            head_split(keys_in),
            preferred_element_type=jnp.float32,
        )
        + bias_grid
    )
    return jnp.where(allowed[None], scores, masked_score)


def attend(queries, keys_in, values, bias_grid, allowed):
    scores = score_block(queries, keys_in, bias_grid, allowed)
    largest = jnp.max(scores, axis=2, keepdims=True)
    weights = jnp.exp(scores - largest)
    totals = jnp.sum(weights, axis=2, keepdims=True)
    probs_low = (weights / totals).astype(jnp.bfloat16)
    mixed_heads = jnp.einsum(
        "hij,jhd->ihd", probs_low, head_split(values), preferred_element_type=jnp.float32
    )
    return (
        mixed_heads.reshape(queries.shape[0], D).astype(jnp.bfloat16),
        largest + jnp.log(totals),
    )


def attend_back(queries, keys_in, values, bias_grid, allowed, log_totals, grad_mixed):
    scores = score_block(queries, keys_in, bias_grid, allowed)
    probs = jnp.exp(scores - log_totals)
    grad_heads = head_split(grad_mixed)
    grad_values = jnp.einsum(
        "hij,ihd->jhd", probs.astype(jnp.bfloat16), grad_heads, preferred_element_type=jnp.float32
    )
    grad_probs = jnp.einsum(
        "ihd,jhd->hij", grad_heads, head_split(values), preferred_element_type=jnp.float32
    )
    grad_scores = (
        probs * (grad_probs - jnp.sum(probs * grad_probs, axis=2, keepdims=True))
    ).astype(jnp.bfloat16)
    grad_queries = jnp.einsum(
        "hij,jhd->ihd", grad_scores, head_split(keys_in), preferred_element_type=jnp.float32
    )
    grad_keys = jnp.einsum(
        "hij,ihd->jhd", grad_scores, head_split(queries), preferred_element_type=jnp.float32
    )
    row_count = queries.shape[0]
    key_count = keys_in.shape[0]
    return (
        grad_queries.reshape(row_count, D).astype(jnp.bfloat16),
        grad_keys.reshape(key_count, D).astype(jnp.bfloat16),
        grad_values.reshape(key_count, D).astype(jnp.bfloat16),
        grad_scores,
    )


def layer_forward(weights, hidden_row, encoder_row, seq_segments, seq_buckets, live_rows):
    (
        gain_self,
        gain_cross,
        gain_ffn,
        bias_flat,
        self_query,
        self_key,
        self_value,
        self_out,
        cross_query,
        cross_key,
        cross_value,
        cross_out,
        feed_gate,
        feed_up,
        feed_down,
    ) = weights
    length = hidden_row.shape[0]
    enc_count = encoder_row.shape[0]
    positions = jnp.arange(length, dtype=jnp.int32)
    allowed = (positions[None, :] <= positions[:, None]) & (
        seq_segments[:, None] == seq_segments[None, :]
    )
    cross_allowed = jnp.broadcast_to(
        jnp.arange(enc_count, dtype=jnp.int32)[None, :] < live_rows, (length, enc_count)
    )
    onehot = (seq_buckets[:, None] == jnp.arange(NB, dtype=jnp.int32)[None, :]).astype(jnp.float32)
    bias_table = bias_flat.astype(jnp.float32).reshape(H, NB)
    bias_grid = toeplitz_expand(jnp.dot(bias_table, onehot.T, precision=highest))
    hidden_wide = hidden_row.astype(jnp.float32)
    normed_one = scaled_norm(hidden_wide, gain_self).astype(jnp.bfloat16)
    queries = product(normed_one, self_query).astype(jnp.bfloat16)
    keys_self = product(normed_one, self_key).astype(jnp.bfloat16)
    values_self = product(normed_one, self_value).astype(jnp.bfloat16)
    mixed_self, lse_self = attend(queries, keys_self, values_self, bias_grid, allowed)
    first_sum = hidden_wide + product(mixed_self, self_out)
    normed_two = scaled_norm(first_sum, gain_cross).astype(jnp.bfloat16)
    cross_queries = product(normed_two, cross_query).astype(jnp.bfloat16)
    cross_keys = product(encoder_row, cross_key).astype(jnp.bfloat16)
    cross_values = product(encoder_row, cross_value).astype(jnp.bfloat16)
    mixed_cross, lse_cross = attend(cross_queries, cross_keys, cross_values, 0.0, cross_allowed)
    second_sum = first_sum + product(mixed_cross, cross_out)
    normed_three = scaled_norm(second_sum, gain_ffn).astype(jnp.bfloat16)
    gate_pre = product(normed_three, feed_gate)
    up_pre = product(normed_three, feed_up)
    hidden_units = gated_gelu(gate_pre, up_pre).astype(jnp.bfloat16)
    result = second_sum + product(hidden_units, feed_down)
    stored = (
        allowed,
        cross_allowed,
        onehot,
        bias_grid,
        hidden_wide,
        encoder_row,
        normed_one,
        queries,
        keys_self,
        values_self,
        lse_self,
        mixed_self,
        first_sum,
        normed_two,
        cross_queries,
        cross_keys,
        cross_values,
        lse_cross,
        mixed_cross,
        second_sum,
        normed_three,
        gate_pre,
        up_pre,
        hidden_units,
    )
    return (result, stored)


def layer_backward(weights, stored, grad_out):
    (
        gain_self,
        gain_cross,
        gain_ffn,
        bias_flat,
        self_query,
        self_key,
        self_value,
        self_out,
        cross_query,
        cross_key,
        cross_value,
        cross_out,
        feed_gate,
        feed_up,
        feed_down,
    ) = weights
    (
        allowed,
        cross_allowed,
        onehot,
        bias_grid,
        hidden_wide,
        encoder_row,
        normed_one,
        queries,
        keys_self,
        values_self,
        lse_self,
        mixed_self,
        first_sum,
        normed_two,
        cross_queries,
        cross_keys,
        cross_values,
        lse_cross,
        mixed_cross,
        second_sum,
        normed_three,
        gate_pre,
        up_pre,
        hidden_units,
    ) = stored
    grad_three = grad_out.astype(jnp.bfloat16)
    grad_feed_down = product_left(hidden_units, grad_three)
    grad_units = product_right(grad_three, feed_down)
    unused, pull_gelu = jax.vjp(gated_gelu, gate_pre, up_pre)
    grad_gate_wide, grad_up_wide = pull_gelu(grad_units)
    grad_gate = grad_gate_wide.astype(jnp.bfloat16)
    grad_upward = grad_up_wide.astype(jnp.bfloat16)
    grad_feed_gate = product_left(normed_three, grad_gate)
    grad_feed_up = product_left(normed_three, grad_upward)
    grad_normed_three = product_right(grad_gate, feed_gate) + product_right(grad_upward, feed_up)
    unused, pull_three = jax.vjp(scaled_norm, second_sum, gain_ffn.astype(jnp.float32))
    grad_from_three, grad_gain_ffn = pull_three(grad_normed_three)
    grad_second = grad_out + grad_from_three
    grad_two = grad_second.astype(jnp.bfloat16)
    grad_cross_out = product_left(mixed_cross, grad_two)
    grad_mixed_cross = product_right(grad_two, cross_out).astype(jnp.bfloat16)
    grad_cq, grad_ck, grad_cv, unused_scores = attend_back(
        cross_queries, cross_keys, cross_values, 0.0, cross_allowed, lse_cross, grad_mixed_cross
    )
    grad_cross_query = product_left(normed_two, grad_cq)
    grad_cross_key = product_left(encoder_row, grad_ck)
    grad_cross_value = product_left(encoder_row, grad_cv)
    grad_encoder_row = product_right(grad_ck, cross_key) + product_right(grad_cv, cross_value)
    grad_normed_two = product_right(grad_cq, cross_query)
    unused, pull_two = jax.vjp(scaled_norm, first_sum, gain_cross.astype(jnp.float32))
    grad_from_two, grad_gain_cross = pull_two(grad_normed_two)
    grad_first = grad_second + grad_from_two
    grad_one = grad_first.astype(jnp.bfloat16)
    grad_self_out = product_left(mixed_self, grad_one)
    grad_mixed_self = product_right(grad_one, self_out).astype(jnp.bfloat16)
    grad_sq, grad_sk, grad_sv, grad_scores = attend_back(
        queries, keys_self, values_self, bias_grid, allowed, lse_self, grad_mixed_self
    )
    grad_offsets = toeplitz_fold(grad_scores.astype(jnp.float32))
    grad_bias = jnp.dot(grad_offsets, onehot, precision=highest).reshape(H * NB)
    grad_self_query = product_left(normed_one, grad_sq)
    grad_self_key = product_left(normed_one, grad_sk)
    grad_self_value = product_left(normed_one, grad_sv)
    grad_normed_one = (
        product_right(grad_sq, self_query)
        + product_right(grad_sk, self_key)
        + product_right(grad_sv, self_value)
    )
    unused, pull_one = jax.vjp(scaled_norm, hidden_wide, gain_self.astype(jnp.float32))
    grad_from_one, grad_gain_self = pull_one(grad_normed_one)
    grad_input = grad_first + grad_from_one
    grads = (
        grad_gain_self,
        grad_gain_cross,
        grad_gain_ffn,
        grad_bias,
        grad_self_query,
        grad_self_key,
        grad_self_value,
        grad_self_out,
        grad_cross_query,
        grad_cross_key,
        grad_cross_value,
        grad_cross_out,
        grad_feed_gate,
        grad_feed_up,
        grad_feed_down,
    )
    return (grad_input, grad_encoder_row, grads)


def body(
    hidden,
    encoder,
    cotangent,
    segment_ids,
    rel_buckets,
    enc_rows,
    dealing,
    gain_self,
    gain_cross,
    gain_ffn,
    rel_bias,
    self_query,
    self_key,
    self_value,
    self_out,
    cross_query,
    cross_key,
    cross_value,
    cross_out,
    feed_gate,
    feed_up,
    feed_down,
):
    device = lax.axis_index("fsdp")
    per_device = cotangent.shape[1]
    micro_count = hidden.shape[0]
    outputs = []
    grad_inputs = []
    grad_encoders = []
    totals = None
    for micro_step in range(micro_count):
        given_order = dealing[micro_step]
        my_slots = lax.dynamic_slice_in_dim(given_order, device * per_device, per_device)
        spread_hidden, spread_encoder = (
            lax.all_to_all(hidden[micro_step], "fsdp", split_axis=1, concat_axis=0, tiled=True),
            lax.all_to_all(encoder[micro_step], "fsdp", split_axis=1, concat_axis=0, tiled=True),
        )
        sorted_hidden = jnp.take(spread_hidden, given_order, axis=0)
        sorted_encoder = jnp.take(spread_encoder, given_order, axis=0)
        dealt_hidden, dealt_encoder = (
            lax.all_to_all(sorted_hidden, "fsdp", split_axis=0, concat_axis=1, tiled=True),
            lax.all_to_all(sorted_encoder, "fsdp", split_axis=0, concat_axis=1, tiled=True),
        )
        weights_fwd = (
            lax.all_gather(gain_self, "fsdp", axis=0, tiled=True),
            lax.all_gather(gain_cross, "fsdp", axis=0, tiled=True),
            lax.all_gather(gain_ffn, "fsdp", axis=0, tiled=True),
            lax.all_gather(rel_bias, "fsdp", axis=0, tiled=True),
            lax.all_gather(self_query, "fsdp", axis=0, tiled=True),
            lax.all_gather(self_key, "fsdp", axis=0, tiled=True),
            lax.all_gather(self_value, "fsdp", axis=0, tiled=True),
            lax.all_gather(self_out, "fsdp", axis=0, tiled=True),
            lax.all_gather(cross_query, "fsdp", axis=0, tiled=True),
            lax.all_gather(cross_key, "fsdp", axis=0, tiled=True),
            lax.all_gather(cross_value, "fsdp", axis=0, tiled=True),
            lax.all_gather(cross_out, "fsdp", axis=0, tiled=True),
            lax.all_gather(feed_gate, "fsdp", axis=0, tiled=True),
            lax.all_gather(feed_up, "fsdp", axis=0, tiled=True),
            lax.all_gather(feed_down, "fsdp", axis=0, tiled=True),
        )
        item_segments = jnp.take(segment_ids[micro_step], my_slots, axis=0)
        item_buckets = jnp.take(rel_buckets[micro_step], my_slots, axis=0)
        item_live = jnp.take(enc_rows[micro_step], my_slots, axis=0)

        def forward_one(packed):
            return layer_forward(weights_fwd, packed[0], packed[1], packed[2], packed[3], packed[4])

        results, stored = lax.map(
            forward_one, (dealt_hidden, dealt_encoder, item_segments, item_buckets, item_live)
        )
        outputs.append(results.astype(jnp.bfloat16))
        weights_bwd = (
            lax.all_gather(gain_self, "fsdp", axis=0, tiled=True),
            lax.all_gather(gain_cross, "fsdp", axis=0, tiled=True),
            lax.all_gather(gain_ffn, "fsdp", axis=0, tiled=True),
            lax.all_gather(rel_bias, "fsdp", axis=0, tiled=True),
            lax.all_gather(self_query, "fsdp", axis=0, tiled=True),
            lax.all_gather(self_key, "fsdp", axis=0, tiled=True),
            lax.all_gather(self_value, "fsdp", axis=0, tiled=True),
            lax.all_gather(self_out, "fsdp", axis=0, tiled=True),
            lax.all_gather(cross_query, "fsdp", axis=0, tiled=True),
            lax.all_gather(cross_key, "fsdp", axis=0, tiled=True),
            lax.all_gather(cross_value, "fsdp", axis=0, tiled=True),
            lax.all_gather(cross_out, "fsdp", axis=0, tiled=True),
            lax.all_gather(feed_gate, "fsdp", axis=0, tiled=True),
            lax.all_gather(feed_up, "fsdp", axis=0, tiled=True),
            lax.all_gather(feed_down, "fsdp", axis=0, tiled=True),
        )

        def backward_step(running, packed):
            grad_input, grad_encoder_row, grads = layer_backward(weights_bwd, packed[0], packed[1])
            running = tuple((earlier + later for earlier, later in zip(running, grads)))
            return (running, (grad_input, grad_encoder_row))

        zero_grads = tuple((jnp.zeros(weight.shape, jnp.float32) for weight in weights_bwd))
        grad_sums, (grad_dealt, grad_enc_dealt) = lax.scan(
            backward_step, zero_grads, (stored, cotangent[micro_step].astype(jnp.float32))
        )
        spread_grad, spread_grad_enc = (
            lax.all_to_all(
                grad_dealt.astype(jnp.bfloat16), "fsdp", split_axis=1, concat_axis=0, tiled=True
            ).astype(grad_dealt.dtype),
            lax.all_to_all(
                grad_enc_dealt.astype(jnp.bfloat16), "fsdp", split_axis=1, concat_axis=0, tiled=True
            ).astype(grad_enc_dealt.dtype),
        )
        inverse = jnp.argsort(given_order)
        given_grad = jnp.take(spread_grad, inverse, axis=0)
        given_grad_enc = jnp.take(spread_grad_enc, inverse, axis=0)
        home_grad, home_grad_enc = (
            lax.all_to_all(
                given_grad.astype(jnp.bfloat16), "fsdp", split_axis=0, concat_axis=1, tiled=True
            ).astype(given_grad.dtype),
            lax.all_to_all(
                given_grad_enc.astype(jnp.bfloat16), "fsdp", split_axis=0, concat_axis=1, tiled=True
            ).astype(given_grad_enc.dtype),
        )
        grad_inputs.append(home_grad)
        grad_encoders.append(home_grad_enc)
        pieces = (
            lax.psum_scatter(grad_sums[0], "fsdp", scatter_dimension=0, tiled=True),
            lax.psum_scatter(grad_sums[1], "fsdp", scatter_dimension=0, tiled=True),
            lax.psum_scatter(grad_sums[2], "fsdp", scatter_dimension=0, tiled=True),
            lax.psum_scatter(grad_sums[3], "fsdp", scatter_dimension=0, tiled=True),
            lax.psum_scatter(grad_sums[4], "fsdp", scatter_dimension=0, tiled=True),
            lax.psum_scatter(grad_sums[5], "fsdp", scatter_dimension=0, tiled=True),
            lax.psum_scatter(grad_sums[6], "fsdp", scatter_dimension=0, tiled=True),
            lax.psum_scatter(grad_sums[7], "fsdp", scatter_dimension=0, tiled=True),
            lax.psum_scatter(grad_sums[8], "fsdp", scatter_dimension=0, tiled=True),
            lax.psum_scatter(grad_sums[9], "fsdp", scatter_dimension=0, tiled=True),
            lax.psum_scatter(grad_sums[10], "fsdp", scatter_dimension=0, tiled=True),
            lax.psum_scatter(grad_sums[11], "fsdp", scatter_dimension=0, tiled=True),
            lax.psum_scatter(grad_sums[12], "fsdp", scatter_dimension=0, tiled=True),
            lax.psum_scatter(grad_sums[13], "fsdp", scatter_dimension=0, tiled=True),
            lax.psum_scatter(grad_sums[14], "fsdp", scatter_dimension=0, tiled=True),
        )
        if totals is None:
            totals = tuple(pieces)
        else:
            totals = tuple((earlier + later for earlier, later in zip(totals, pieces)))
    return (jnp.stack(outputs), jnp.stack(grad_inputs), jnp.stack(grad_encoders)) + tuple(totals)


def solution(mesh):
    return jax.shard_map(
        body,
        mesh=mesh,
        in_specs=(
            P(None, "fsdp", None, None),
            P(None, "fsdp", None, None),
            P(None, "fsdp", None, None),
            P(),
            P(),
            P(),
            P(),
            P("fsdp"),
            P("fsdp"),
            P("fsdp"),
            P("fsdp"),
            P("fsdp", None),
            P("fsdp", None),
            P("fsdp", None),
            P("fsdp", None),
            P("fsdp", None),
            P("fsdp", None),
            P("fsdp", None),
            P("fsdp", None),
            P("fsdp", None),
            P("fsdp", None),
            P("fsdp", None),
        ),
        out_specs=(
            P(None, "fsdp", None, None),
            P(None, "fsdp", None, None),
            P(None, "fsdp", None, None),
            P("fsdp"),
            P("fsdp"),
            P("fsdp"),
            P("fsdp"),
            P("fsdp", None),
            P("fsdp", None),
            P("fsdp", None),
            P("fsdp", None),
            P("fsdp", None),
            P("fsdp", None),
            P("fsdp", None),
            P("fsdp", None),
            P("fsdp", None),
            P("fsdp", None),
            P("fsdp", None),
        ),
        check_vma=False,
    )
```

profile of v0, /device:TPU:0, one launch (start us, length us, event | category | flops | bytes accessed | tf_op | source)
XLA Modules:
  0.0 2367.0 jit_solution(3501548552241820163)
XLA Ops:
  33.2 41.0 %all-reduce.11 = (bf16[1024]{0:T(1024)(128)(2,1)S(1)}, bf16[512]{0:T(512)(128)(2,1)S(1)}, bf16[1024]{0:T(1024)(128)(2,1)S(1)}, bf16[1024]{0:T(1024)(128)(2,1)S(1)}) all-reduce(bf16[1024]{0:T(1024)(128)(2,1)S(1)} %dynamic-update-slice.3, bf16[512]{0:T(512)(128)(2,1)S(1)} %dynamic-update-slice.4, ...), channel_id=1, replica_groups=mesh['fsdp'=32] {'fsdp'}, use_global_device_ids=true, to_apply=%add.2 | all-reduce | flops 3584 | bytes 14336
  87.1 8.0 all-to-all-done
  101.5 9.1 all-to-all-done.5
  183.4 9.1 all-gather.12.cloned.1.call-done
  195.4 55.9 %all-gather.18.cloned.1.call-done = bf16[1024,1024]{1,0:T(8,128)(2,1)} async-done(((bf16[32,1024]{1,0:T(8,128)(2,1)}), bf16[1024,1024]{1,0:T(8,128)(2,1)}) %all-gather.18.cloned.1.call-update) | async-done | bytes 2097168 | tf_op jit(solution)/shard_map/all_gather | solution.py:362
  257.3 52.1 %all-gather.20.cloned.1.call-done = bf16[1024,1024]{1,0:T(8,128)(2,1)} async-done(((bf16[32,1024]{1,0:T(8,128)(2,1)}), bf16[1024,1024]{1,0:T(8,128)(2,1)}) %all-gather.20.cloned.1.call-update) | async-done | bytes 2097168 | tf_op jit(solution)/shard_map/all_gather | solution.py:365
  311.7 55.5 %all-gather.24.cloned.1.call-done = bf16[1024,1024]{1,0:T(8,128)(2,1)} async-done(((bf16[32,1024]{1,0:T(8,128)(2,1)}), bf16[1024,1024]{1,0:T(8,128)(2,1)}) %all-gather.24.cloned.1.call-update) | async-done | bytes 2097168 | tf_op jit(solution)/shard_map/all_gather | solution.py:364
  370.3 54.8 %all-gather.22.cloned.1.call-done = bf16[1024,1024]{1,0:T(8,128)(2,1)} async-done(((bf16[32,1024]{1,0:T(8,128)(2,1)}), bf16[1024,1024]{1,0:T(8,128)(2,1)}) %all-gather.22.cloned.1.call-update) | async-done | bytes 2097168 | tf_op jit(solution)/shard_map/all_gather | solution.py:363
  465.2 17.8 all-gather.26.cloned.1.call-done
  490.1 62.0 %all-gather.28.cloned.1.call-done = bf16[1024,2816]{1,0:T(8,128)(2,1)} async-done(((bf16[32,2816]{1,0:T(8,128)(2,1)}), bf16[1024,2816]{1,0:T(8,128)(2,1)}) %all-gather.28.cloned.1.call-update) | async-done | bytes 5767184 | tf_op jit(solution)/shard_map/all_gather | solution.py:367
  556.8 64.0 %all-gather.30.cloned.1.call-done = bf16[1024,2816]{1,0:T(8,128)(2,1)} async-done(((bf16[32,2816]{1,0:T(8,128)(2,1)}), bf16[1024,2816]{1,0:T(8,128)(2,1)}) %all-gather.30.cloned.1.call-update) | async-done | bytes 5767184 | tf_op jit(solution)/shard_map/all_gather | solution.py:368
  625.5 64.1 %all-gather.32.cloned.1.call-done = bf16[2816,1024]{1,0:T(8,128)(2,1)} async-done(((bf16[88,1024]{1,0:T(8,128)(2,1)}), bf16[2816,1024]{1,0:T(8,128)(2,1)}) %all-gather.32.cloned.1.call-update) | async-done | bytes 5767184 | tf_op jit(solution)/shard_map/all_gather | solution.py:369
  934.0 9.2 all-to-all-done.12
  955.4 41.2 %all-reduce.10 = (f32[1024]{0:T(1024)S(1)}, f32[1024]{0:T(1024)S(1)}, f32[1024]{0:T(1024)S(1)}, f32[512]{0:T(512)S(1)}) all-reduce(f32[1024]{0:T(1024)S(1)} %add.540, f32[1024]{0:T(1024)S(1)} %add.541, f32[1024]{0:T(1024)S(1)} %add.542, f32[512]{0:T(512)S(1)} %reshape.1165), channel_id=17, replica_groups=mesh['fsdp'=32] {'fsdp'}, use_global_device_ids=true, to_apply=%region_27.33.clone | all-reduce | flops 3584 | bytes 28672
  1025.5 19.1 reduce-scatter.14.cloned.1.call-done
  1044.6 142.1 %reduce-scatter.16.cloned.1.call-done = f32[32,1024]{1,0:T(8,128)} async-done(((f32[1024,1024]{1,0:T(8,128)}), f32[32,1024]{1,0:T(8,128)}) %reduce-scatter.16.cloned.1.call-update) | async-done | bytes 131088 | tf_op jit(solution)/shard_map/reduce_scatter | solution.py:437
  1186.7 141.2 %reduce-scatter.18.cloned.1.call-done = f32[32,1024]{1,0:T(8,128)} async-done(((f32[1024,1024]{1,0:T(8,128)}), f32[32,1024]{1,0:T(8,128)}) %reduce-scatter.18.cloned.1.call-update) | async-done | bytes 131088 | tf_op jit(solution)/shard_map/reduce_scatter | solution.py:438
  1327.9 141.7 %reduce-scatter.20.cloned.1.call-done = f32[32,1024]{1,0:T(8,128)} async-done(((f32[1024,1024]{1,0:T(8,128)}), f32[32,1024]{1,0:T(8,128)}) %reduce-scatter.20.cloned.1.call-update) | async-done | bytes 131088 | tf_op jit(solution)/shard_map/reduce_scatter | solution.py:439
  1469.5 141.6 %reduce-scatter.22.cloned.1.call-done = f32[32,1024]{1,0:T(8,128)} async-done(((f32[1024,1024]{1,0:T(8,128)}), f32[32,1024]{1,0:T(8,128)}) %reduce-scatter.22.cloned.1.call-update) | async-done | bytes 131088 | tf_op jit(solution)/shard_map/reduce_scatter | solution.py:440
  1611.1 141.5 %reduce-scatter.24.cloned.1.call-done = f32[32,1024]{1,0:T(8,128)} async-done(((f32[1024,1024]{1,0:T(8,128)}), f32[32,1024]{1,0:T(8,128)}) %reduce-scatter.24.cloned.1.call-update) | async-done | bytes 131088 | tf_op jit(solution)/shard_map/reduce_scatter | solution.py:441
  1752.6 141.6 %reduce-scatter.26.cloned.1.call-done = f32[32,1024]{1,0:T(8,128)} async-done(((f32[1024,1024]{1,0:T(8,128)}), f32[32,1024]{1,0:T(8,128)}) %reduce-scatter.26.cloned.1.call-update) | async-done | bytes 131088 | tf_op jit(solution)/shard_map/reduce_scatter | solution.py:442
  1894.3 155.1 %reduce-scatter.28.cloned.1.call-done = f32[32,2816]{1,0:T(8,128)} async-done(((f32[1024,2816]{1,0:T(8,128)}), f32[32,2816]{1,0:T(8,128)}) %reduce-scatter.28.cloned.1.call-update) | async-done | bytes 360464 | tf_op jit(solution)/shard_map/reduce_scatter | solution.py:443
  2049.4 155.2 %reduce-scatter.30.cloned.1.call-done = f32[32,2816]{1,0:T(8,128)} async-done(((f32[1024,2816]{1,0:T(8,128)}), f32[32,2816]{1,0:T(8,128)}) %reduce-scatter.30.cloned.1.call-update) | async-done | bytes 360464 | tf_op jit(solution)/shard_map/reduce_scatter | solution.py:444
  2204.6 155.2 %reduce-scatter.32.cloned.1.call-done = f32[88,1024]{1,0:T(8,128)} async-done(((f32[2816,1024]{1,0:T(8,128)}), f32[88,1024]{1,0:T(8,128)}) %reduce-scatter.32.cloned.1.call-update) | async-done | bytes 360464 | tf_op jit(solution)/shard_map/reduce_scatter | solution.py:445
  (701 shorter events, 467.4 us)
Async XLA Ops:
  7.2 169.9 %all-gather.14.cloned.1.call-start = ((), (), s32[]{:S(2)}) async-start(), calls=%async_computation.28 | async-start | bytes 2162688 | tf_op jit(solution)/shard_map/all_gather | solution.py:359
  7.9 171.4 %all-gather.16.cloned.1.call-start = ((), (), s32[]{:S(2)}) async-start(), calls=%async_computation.29 | async-start | bytes 2162688 | tf_op jit(solution)/shard_map/all_gather | solution.py:360
  8.7 183.8 %all-gather.12.cloned.1.call-start = ((), (), s32[]{:S(2)}) async-start(), calls=%async_computation.27 | async-start | bytes 2162688 | tf_op jit(solution)/shard_map/all_gather | solution.py:361
  9.4 241.9 %all-gather.18.cloned.1.call-start = ((), (), s32[]{:S(2)}) async-start(), calls=%async_computation.30 | async-start | bytes 2162688 | tf_op jit(solution)/shard_map/all_gather | solution.py:362
  10.0 299.4 %all-gather.20.cloned.1.call-start = ((), (), s32[]{:S(2)}) async-start(), calls=%async_computation.31 | async-start | bytes 2162688 | tf_op jit(solution)/shard_map/all_gather | solution.py:365
  10.6 356.6 %all-gather.24.cloned.1.call-start = ((), (), s32[]{:S(2)}) async-start(), calls=%async_computation.33 | async-start | bytes 2162688 | tf_op jit(solution)/shard_map/all_gather | solution.py:364
  11.1 414.0 %all-gather.22.cloned.1.call-start = ((), (), s32[]{:S(2)}) async-start(), calls=%async_computation.32 | async-start | bytes 2162688 | tf_op jit(solution)/shard_map/all_gather | solution.py:363
  11.9 471.2 %all-gather.26.cloned.1.call-start = ((), (), s32[]{:S(2)}) async-start(), calls=%async_computation.34 | async-start | bytes 2162688 | tf_op jit(solution)/shard_map/all_gather | solution.py:366
  12.7 539.5 %all-gather.28.cloned.1.call-start = ((), (), s32[]{:S(2)}) async-start(), calls=%async_computation.35 | async-start | bytes 5947392 | tf_op jit(solution)/shard_map/all_gather | solution.py:367
  13.4 607.4 %all-gather.30.cloned.1.call-start = ((), (), s32[]{:S(2)}) async-start(), calls=%async_computation.36 | async-start | bytes 5947392 | tf_op jit(solution)/shard_map/all_gather | solution.py:368
  26.5 663.2 %all-gather.32.cloned.1.call-start = ((), (), s32[]{:S(2)}) async-start(), calls=%async_computation.37 | async-start | bytes 5947392 | tf_op jit(solution)/shard_map/all_gather | solution.py:369
  166.4 87.0 %all-to-all-start.7 = ((bf16[32,8,1024]{2,1,0:T(8,128)(2,1)}), bf16[32,8,1024]{2,1,0:T(8,128)(2,1)S(1)}, u32[]{:S(2)}, u32[]{:S(2)}) async-start(bf16[32,8,1024]{2,1,0:T(8,128)(2,1)} %broadcast_select_fusion), calls=%async_computation.7 | async-start | bytes 1048576 | tf_op jit(solution)/shard_map/all_to_all | solution.py:352
  253.5 190.0 %all-to-all-start.3 = ((bf16[32,8,1024]{2,1,0:T(8,128)(2,1)}), bf16[32,8,1024]{2,1,0:T(8,128)(2,1)}, u32[]{:S(2)}, u32[]{:S(2)}) async-start(bf16[32,8,1024]{2,1,0:T(8,128)(2,1)} %broadcast_select_fusion.1), calls=%async_computation.3 | async-start | bytes 1048576 | tf_op jit(solution)/shard_map/all_to_all | solution.py:352
  257.1 768.4 %reduce-scatter.12.cloned.1.call-start = ((), (), s32[]{:S(2)}) async-start(), calls=%async_computation.38 | async-start | bytes 4325376 | tf_op jit(solution)/shard_map/reduce_scatter | solution.py:435
  754.5 290.0 %reduce-scatter.14.cloned.1.call-start = ((), (), s32[]{:S(2)}) async-start(), calls=%async_computation.39 | async-start | bytes 4325376 | tf_op jit(solution)/shard_map/reduce_scatter | solution.py:436
  761.9 424.8 %reduce-scatter.16.cloned.1.call-start = ((), (), s32[]{:S(2)}) async-start(), calls=%async_computation.40 | async-start | bytes 4325376 | tf_op jit(solution)/shard_map/reduce_scatter | solution.py:437
  768.9 558.9 %reduce-scatter.18.cloned.1.call-start = ((), (), s32[]{:S(2)}) async-start(), calls=%async_computation.41 | async-start | bytes 4325376 | tf_op jit(solution)/shard_map/reduce_scatter | solution.py:438
  774.4 695.2 %reduce-scatter.20.cloned.1.call-start = ((), (), s32[]{:S(2)}) async-start(), calls=%async_computation.42 | async-start | bytes 4325376 | tf_op jit(solution)/shard_map/reduce_scatter | solution.py:439
  780.0 831.2 %reduce-scatter.22.cloned.1.call-start = ((), (), s32[]{:S(2)}) async-start(), calls=%async_computation.43 | async-start | bytes 4325376 | tf_op jit(solution)/shard_map/reduce_scatter | solution.py:440
  788.6 964.0 %reduce-scatter.24.cloned.1.call-start = ((), (), s32[]{:S(2)}) async-start(), calls=%async_computation.44 | async-start | bytes 4325376 | tf_op jit(solution)/shard_map/reduce_scatter | solution.py:441
  796.5 1097.8 %reduce-scatter.26.cloned.1.call-start = ((), (), s32[]{:S(2)}) async-start(), calls=%async_computation.45 | async-start | bytes 4325376 | tf_op jit(solution)/shard_map/reduce_scatter | solution.py:442
  801.0 1248.4 %reduce-scatter.28.cloned.1.call-start = ((), (), s32[]{:S(2)}) async-start(), calls=%async_computation.46 | async-start | bytes 11894784 | tf_op jit(solution)/shard_map/reduce_scatter | solution.py:443
  809.8 1394.8 %reduce-scatter.30.cloned.1.call-start = ((), (), s32[]{:S(2)}) async-start(), calls=%async_computation.47 | async-start | bytes 11894784 | tf_op jit(solution)/shard_map/reduce_scatter | solution.py:444
  818.5 1541.2 %reduce-scatter.32.cloned.1.call-start = ((), (), s32[]{:S(2)}) async-start(), calls=%async_computation.48 | async-start | bytes 11894784 | tf_op jit(solution)/shard_map/reduce_scatter | solution.py:445
  (177 other events, 1613.1 us)
Sparse Core Ops, SparseCore 0:
  10.9 59.9 all-gather.13
  73.7 58.4 all-gather.15
  135.1 57.2 all-gather.11
  195.2 56.0 all-gather.17
  254.0 55.3 all-gather.19
  312.1 55.0 all-gather.23
  370.0 55.0 all-gather.21
  428.0 55.0 all-gather.25
  485.9 66.1 all-gather.27
  554.8 65.9 all-gather.29
  623.7 65.9 all-gather.31
  754.7 144.3 reduce-scatter.11
  901.9 142.6 reduce-scatter.13
  1047.3 139.3 reduce-scatter.15
  1189.4 138.4 reduce-scatter.17
  1330.6 138.9 reduce-scatter.19
  1472.2 138.8 reduce-scatter.21
  1613.8 138.7 reduce-scatter.23
  1755.5 138.7 reduce-scatter.25
  1897.0 152.3 reduce-scatter.27
  2052.3 152.2 reduce-scatter.29
  2207.5 152.2 reduce-scatter.31
where the time goes:
time: 2380 us; the launch traced here: 2370 us
  waiting for transfers between devices  1850 us (78%)
  matrix products  179 us (8%)
  local copies, waits for them, and re-layouts  114 us (5%)
  blocking collectives  82.2 us (3%)
  starting transfers between devices  63.5 us (3%)
  other arithmetic  57.2 us (2%)
    reduce_scatter x1, waiting for transfers between devices, body(): lax.psum_scatter(grad_sums[13], 'fsdp', scatter_dimension=0, tiled=True)  155 us
    reduce_scatter x1, waiting for transfers between devices, body(): lax.psum_scatter(grad_sums[14], 'fsdp', scatter_dimension=0, tiled=True)  155 us
    reduce_scatter x1, waiting for transfers between devices, body(): lax.psum_scatter(grad_sums[12], 'fsdp', scatter_dimension=0, tiled=True)  155 us
    reduce_scatter x1, waiting for transfers between devices, body(): lax.psum_scatter(grad_sums[6], 'fsdp', scatter_dimension=0, tiled=True)  142 us
    reduce_scatter x1, waiting for transfers between devices, body(): lax.psum_scatter(grad_sums[8], 'fsdp', scatter_dimension=0, tiled=True)  142 us
    reduce_scatter x1, waiting for transfers between devices, body(): lax.psum_scatter(grad_sums[11], 'fsdp', scatter_dimension=0, tiled=True)  142 us
    reduce_scatter x1, waiting for transfers between devices, body(): lax.psum_scatter(grad_sums[9], 'fsdp', scatter_dimension=0, tiled=True)  142 us
    reduce_scatter x1, waiting for transfers between devices, body(): lax.psum_scatter(grad_sums[10], 'fsdp', scatter_dimension=0, tiled=True)  142 us
  transfers between devices with their start and end apart: 38, of which 30 were waited for; matrix products, arithmetic and copies ran while one was open for 11% of the time, Pallas kernels for 0%

commit v1 on v0

v1 whole, which is shorter than its diff:
```python
import jax
import jax.numpy as jnp
from jax import lax
from jax.sharding import PartitionSpec as P

D = 1024
H = 16
DH = 64
NB = 32

AXIS = "fsdp"
eps_norm = 1e-06
masked_score = -1000000000.0
highest = lax.Precision.HIGHEST
f32 = jnp.float32
bf16 = jnp.bfloat16


def product(left_side, right_side):
    return jnp.dot(left_side, right_side, preferred_element_type=f32)


def product_left(left_side, right_side):
    return lax.dot_general(
        left_side, right_side, (((0,), (0,)), ((), ())), preferred_element_type=f32
    )


def product_right(left_side, right_side):
    return lax.dot_general(
        left_side, right_side, (((1,), (1,)), ((), ())), preferred_element_type=f32
    )


def inverse_rms(values):
    return lax.rsqrt(jnp.mean(values * values, axis=-1, keepdims=True) + eps_norm)


def norm_back(values, inverse, gain_row, grad):
    scaled = values * inverse
    weighted = grad * gain_row
    centre = jnp.mean(weighted * scaled, axis=-1, keepdims=True)
    return inverse * (weighted - scaled * centre), jnp.sum(grad * scaled, axis=0)


def gelu_parts(gate_pre):
    root = 0.7978845608028654
    inner = root * (gate_pre + 0.044715 * gate_pre * gate_pre * gate_pre)
    curve = jnp.tanh(inner)
    value = 0.5 * gate_pre * (1.0 + curve)
    slope = 0.5 * (1.0 + curve) + 0.5 * gate_pre * (1.0 - curve * curve) * root * (
        1.0 + 3 * 0.044715 * gate_pre * gate_pre
    )
    return value, slope


def toeplitz_expand(per_offset):
    head_count, length = per_offset.shape
    filler = jnp.zeros((head_count, 1), f32)
    pattern = jnp.concatenate(
        [per_offset[:, :1], filler, per_offset[:, ::-1][:, : length - 1]], axis=1
    )
    tiled_rows = jnp.broadcast_to(pattern[:, None, :], (head_count, length, length + 1))
    return tiled_rows.reshape(head_count, length * (length + 1))[:, : length * length].reshape(
        head_count, length, length
    )


def toeplitz_fold(score_grid):
    head_count, length = (score_grid.shape[0], score_grid.shape[1])
    flat_grid = score_grid.reshape(head_count, length * length)
    padded = jnp.concatenate([flat_grid, jnp.zeros((head_count, length), f32)], axis=1)
    columns = jnp.sum(padded.reshape(head_count, length, length + 1), axis=1)
    return jnp.concatenate([columns[:, :1], columns[:, 2:][:, ::-1]], axis=1)


def heads(matrix, blocks):
    return matrix.reshape(blocks, -1, H, DH)


def score_block(queries, keys_in, bias_grid, allowed):
    scores = jnp.einsum("bihd,bjhd->bhij", queries, keys_in, preferred_element_type=f32)
    if bias_grid is not None:
        scores = scores + bias_grid
    return jnp.where(allowed[:, None], scores, masked_score)


def attend(queries, keys_in, values, bias_grid, allowed):
    blocks = allowed.shape[0]
    scores = score_block(heads(queries, blocks), heads(keys_in, blocks), bias_grid, allowed)
    largest = jnp.max(scores, axis=3, keepdims=True)
    weights = jnp.exp(scores - largest)
    probs = weights / jnp.sum(weights, axis=3, keepdims=True)
    mixed = jnp.einsum(
        "bhij,bjhd->bihd", probs.astype(bf16), heads(values, blocks), preferred_element_type=f32
    )
    return mixed.reshape(queries.shape[0], D).astype(bf16), probs


def attend_back(queries, keys_in, values, probs, grad_mixed):
    blocks = probs.shape[0]
    grad_heads = heads(grad_mixed, blocks)
    grad_values = jnp.einsum(
        "bhij,bihd->bjhd", probs.astype(bf16), grad_heads, preferred_element_type=f32
    )
    grad_probs = jnp.einsum(
        "bihd,bjhd->bhij", grad_heads, heads(values, blocks), preferred_element_type=f32
    )
    grad_scores = (
        probs * (grad_probs - jnp.sum(probs * grad_probs, axis=3, keepdims=True))
    ).astype(bf16)
    grad_queries = jnp.einsum(
        "bhij,bjhd->bihd", grad_scores, heads(keys_in, blocks), preferred_element_type=f32
    )
    grad_keys = jnp.einsum(
        "bhij,bihd->bjhd", grad_scores, heads(queries, blocks), preferred_element_type=f32
    )
    return (
        grad_queries.reshape(-1, D).astype(bf16),
        grad_keys.reshape(-1, D).astype(bf16),
        grad_values.reshape(-1, D).astype(bf16),
        grad_scores,
    )


def redeal(blocks, source):
    micro, own, rows, width = blocks.shape
    count = source.shape[1] // own
    cut = blocks.reshape(micro, own, count, rows // count, width).transpose(2, 0, 1, 3, 4)
    spread = lax.all_to_all(cut, AXIS, split_axis=0, concat_axis=0, tiled=True)
    spread = spread.transpose(1, 0, 2, 3, 4).reshape(micro, count * own, rows // count, width)
    moved = jnp.take_along_axis(spread, source[:, :, None, None], axis=1)
    moved = moved.reshape(micro, count, own, rows // count, width).transpose(1, 0, 2, 3, 4)
    home = lax.all_to_all(moved, AXIS, split_axis=0, concat_axis=0, tiled=True)
    return home.transpose(1, 2, 0, 3, 4).reshape(micro, own, rows, width)


def gather_weights(wide, deep):
    packed = lax.all_gather(jnp.concatenate(wide, axis=1), AXIS, axis=0, tiled=True)
    whole, start = [], 0
    for part in wide:
        whole.append(packed[:, start : start + part.shape[1]])
        start += part.shape[1]
    return whole, lax.all_gather(deep, AXIS, axis=0, tiled=True)


def scatter_grads(wide, deep):
    packed = jnp.concatenate([part.astype(bf16) for part in wide], axis=1)
    packed = lax.psum_scatter(packed, AXIS, scatter_dimension=0, tiled=True).astype(f32)
    pieces, start = [], 0
    for part in wide:
        pieces.append(packed[:, start : start + part.shape[1]])
        start += part.shape[1]
    deep = lax.psum_scatter(deep.astype(bf16), AXIS, scatter_dimension=0, tiled=True)
    return pieces, deep.astype(f32)


def body(
    hidden,
    encoder,
    cotangent,
    segment_ids,
    rel_buckets,
    enc_rows,
    dealing,
    gain_self,
    gain_cross,
    gain_ffn,
    rel_bias,
    self_query,
    self_key,
    self_value,
    self_out,
    cross_query,
    cross_key,
    cross_value,
    cross_out,
    feed_gate,
    feed_up,
    feed_down,
):
    device = lax.axis_index(AXIS)
    micro, own, length, _ = hidden.shape
    enc_count = encoder.shape[2]
    blocks = micro * own
    first = device * own

    def mine(table):
        return lax.dynamic_slice_in_dim(table, first, own, axis=1).reshape(
            (blocks,) + table.shape[2:]
        )

    segments, buckets, live = mine(segment_ids), mine(rel_buckets), mine(enc_rows)
    grad_out = redeal(cotangent, jnp.argsort(dealing, axis=1)).reshape(blocks * length, D)

    small = jnp.concatenate([gain_self, gain_cross, gain_ffn, rel_bias])
    smalls = lax.all_gather(small, AXIS, axis=0)
    part = gain_self.shape[0]
    gain_one, gain_two, gain_three = [
        smalls[:, k * part : (k + 1) * part].reshape(D).astype(f32) for k in range(3)
    ]
    bias_table = smalls[:, 3 * part :].reshape(H, NB).astype(f32)
    (wq, wk, wv, wo, xq, xk, xv, xo, gate, up), down = gather_weights(
        (
            self_query,
            self_key,
            self_value,
            self_out,
            cross_query,
            cross_key,
            cross_value,
            cross_out,
            feed_gate,
            feed_up,
        ),
        feed_down,
    )

    positions = jnp.arange(length, dtype=jnp.int32)
    allowed = (positions[None, :] <= positions[:, None])[None] & (
        segments[:, :, None] == segments[:, None, :]
    )
    cross_allowed = jnp.broadcast_to(
        jnp.arange(enc_count, dtype=jnp.int32)[None, None, :] < live[:, None, None],
        (blocks, length, enc_count),
    )
    onehot = (buckets[:, :, None] == jnp.arange(NB, dtype=jnp.int32)).astype(f32)
    per_offset = jnp.einsum("hc,boc->bho", bias_table, onehot, precision=highest)
    bias_grid = toeplitz_expand(per_offset.reshape(blocks * H, length)).reshape(
        blocks, H, length, length
    )

    wide_in = hidden.reshape(blocks * length, D).astype(f32)
    enc_in = encoder.reshape(blocks * enc_count, D)
    inv_one = inverse_rms(wide_in)
    normed_one = (wide_in * inv_one * gain_one).astype(bf16)
    queries = product(normed_one, wq).astype(bf16)
    keys_self = product(normed_one, wk).astype(bf16)
    values_self = product(normed_one, wv).astype(bf16)
    mixed_self, probs_self = attend(queries, keys_self, values_self, bias_grid, allowed)
    first_sum = wide_in + product(mixed_self, wo)
    inv_two = inverse_rms(first_sum)
    normed_two = (first_sum * inv_two * gain_two).astype(bf16)
    cross_queries = product(normed_two, xq).astype(bf16)
    cross_keys = product(enc_in, xk).astype(bf16)
    cross_values = product(enc_in, xv).astype(bf16)
    mixed_cross, probs_cross = attend(
        cross_queries, cross_keys, cross_values, None, cross_allowed
    )
    second_sum = first_sum + product(mixed_cross, xo)
    inv_three = inverse_rms(second_sum)
    normed_three = (second_sum * inv_three * gain_three).astype(bf16)
    gate_pre = product(normed_three, gate)
    up_pre = product(normed_three, up)
    act, slope = gelu_parts(gate_pre)
    hidden_units = (act * up_pre).astype(bf16)
    result = (second_sum + product(hidden_units, down)).astype(bf16)
    layer_out = redeal(result.reshape(micro, own, length, D), dealing)

    g_down = product_left(hidden_units, grad_out)
    grad_units = product_right(grad_out, down)
    grad_gate = (grad_units * up_pre * slope).astype(bf16)
    grad_up = (grad_units * act).astype(bf16)
    g_gate = product_left(normed_three, grad_gate)
    g_up = product_left(normed_three, grad_up)
    grad_three = product_right(grad_gate, gate) + product_right(grad_up, up)
    back, g_gain_three = norm_back(second_sum, inv_three, gain_three, grad_three)
    grad_second = grad_out.astype(f32) + back
    grad_low = grad_second.astype(bf16)
    g_xo = product_left(mixed_cross, grad_low)
    grad_mixed = product_right(grad_low, xo).astype(bf16)
    grad_cq, grad_ck, grad_cv, _ = attend_back(
        cross_queries, cross_keys, cross_values, probs_cross, grad_mixed
    )
    g_xq = product_left(normed_two, grad_cq)
    g_xk = product_left(enc_in, grad_ck)
    g_xv = product_left(enc_in, grad_cv)
    grad_enc = product_right(grad_ck, xk) + product_right(grad_cv, xv)
    back, g_gain_two = norm_back(first_sum, inv_two, gain_two, product_right(grad_cq, xq))
    grad_first = grad_second + back
    grad_low = grad_first.astype(bf16)
    g_so = product_left(mixed_self, grad_low)
    grad_mixed = product_right(grad_low, wo).astype(bf16)
    grad_sq, grad_sk, grad_sv, grad_scores = attend_back(
        queries, keys_self, values_self, probs_self, grad_mixed
    )
    offsets = toeplitz_fold(
        grad_scores.astype(f32).reshape(blocks * H, length, length)
    ).reshape(blocks, H, length)
    g_bias = jnp.einsum("bho,boc->hc", offsets, onehot, precision=highest).reshape(H * NB)
    g_sq = product_left(normed_one, grad_sq)
    g_sk = product_left(normed_one, grad_sk)
    g_sv = product_left(normed_one, grad_sv)
    grad_one = (
        product_right(grad_sq, wq) + product_right(grad_sk, wk) + product_right(grad_sv, wv)
    )
    back, g_gain_one = norm_back(wide_in, inv_one, gain_one, grad_one)
    grad_in = grad_first + back

    pieces, piece_down = scatter_grads(
        (g_sq, g_sk, g_sv, g_so, g_xq, g_xk, g_xv, g_xo, g_gate, g_up), g_down
    )
    count = smalls.shape[0]
    small_grads = jnp.concatenate(
        [g.reshape(count, -1) for g in (g_gain_one, g_gain_two, g_gain_three, g_bias)], axis=1
    )
    small_sum = jnp.sum(
        lax.all_to_all(small_grads, AXIS, split_axis=0, concat_axis=0, tiled=True), axis=0
    )
    return (
        layer_out,
        grad_in.reshape(hidden.shape),
        grad_enc.reshape(encoder.shape),
        small_sum[:part],
        small_sum[part : 2 * part],
        small_sum[2 * part : 3 * part],
        small_sum[3 * part :],
        *pieces,
        piece_down,
    )


def solution(mesh):
    block = P(None, AXIS, None, None)
    row = P(AXIS)
    matrix = P(AXIS, None)
    return jax.shard_map(
        body,
        mesh=mesh,
        in_specs=(block,) * 3 + (P(),) * 4 + (row,) * 4 + (matrix,) * 11,
        out_specs=(block,) * 3 + (row,) * 4 + (matrix,) * 11,
        check_vma=False,
    )
```

time: 2380 us -> 760 us (0.32)
  waiting for transfers between devices: 1850 us -> 371 us
  starting transfers between devices: 63.5 us -> 22.5 us
  blocking collectives: 82.2 us -> 41.3 us
  matrix products: 179 us -> 140 us
  other arithmetic: 57.2 us -> 21.9 us
  local copies, waits for them, and re-layouts: 114 us -> 141 us
    reduce_scatter x11 -> x2, waiting for transfers between devices: 1330 us -> 195 us  [the longest x1 195 us: scatter_grads(): lax.psum_scatter(packed, AXIS, scatter_dimension=0, tiled=True).astype(f32)]
    all_gather x11 -> x2, waiting for transfers between devices: 435 us -> 139 us  [the longest x1 139 us: gather_weights(): lax.all_gather(jnp.concatenate(wide, axis=1), AXIS, axis=0, tiled=True)]
    unnamed x2 -> x1, blocking collectives: 82.2 us -> 41.3 us
    all_to_all x16 -> x5, starting transfers between devices: 61.7 us -> 22.1 us  [the longest x2 10.9 us: redeal(): spread = lax.all_to_all(cut, AXIS, split_axis=0, concat_axis=0, tiled=True)]
    all_to_all x16 -> x5, waiting for transfers between devices: 73.7 us -> 36.2 us  [the longest x2 30.1 us: redeal(): home = lax.all_to_all(moved, AXIS, split_axis=0, concat_axis=0, tiled=True)]
    unnamed x10 -> x0, other arithmetic: 26.6 us -> none
    dot_general x22 -> x11, matrix products: 54.9 us -> 32.6 us  [product_left(): lax.dot_general(left_side, right_side, (((0,), (0,)), ((), ())), preferre...]
    dot_general x50 -> x25, matrix products: 84.8 us -> 65.4 us  [the longest x11 41.3 us: product(): return jnp.dot(left_side, right_side, preferred_element_type=f32)]
  transfers between devices with their start and end apart: 38 -> 9, of which waited for: 30 -> 6; matrix products, arithmetic and copies ran while one was open for 11% -> 29% of each run, Pallas kernels for 0% -> 0%
where the time goes in v1:
time: 760 us; the launch traced here: 752 us
  waiting for transfers between devices  371 us (49%)
  local copies, waits for them, and re-layouts  141 us (19%)
  matrix products  140 us (18%)
  blocking collectives  41.3 us (5%)
  starting transfers between devices  22.5 us (3%)
  other arithmetic  21.9 us (3%)
  between operations  15.3 us (2%)
    reduce_scatter x1, waiting for transfers between devices, scatter_grads(): lax.psum_scatter(packed, AXIS, scatter_dimension=0, tiled=True).astype(f32)  195 us
    all_gather x1, waiting for transfers between devices, gather_weights(): lax.all_gather(jnp.concatenate(wide, axis=1), AXIS, axis=0, tiled=True)  139 us
    unnamed x159, local copies, waits for them, and re-layouts  43.8 us
    dot_general x11, matrix products, product_right(): lax.dot_general(left_side, right_side, (((1,), (1,)), ((), ())), preferre...  41.7 us
    dot_general x11, matrix products, product(): return jnp.dot(left_side, right_side, preferred_element_type=f32)  41.3 us
    unnamed x1, blocking collectives  41.3 us
    dot_general x11, matrix products, product_left(): lax.dot_general(left_side, right_side, (((0,), (0,)), ((), ())), preferre...  32.6 us
    all_to_all x2, waiting for transfers between devices, redeal(): home = lax.all_to_all(moved, AXIS, split_axis=0, concat_axis=0, tiled=True)  30.1 us
  transfers between devices with their start and end apart: 9, of which 6 were waited for; matrix products, arithmetic and copies ran while one was open for 29% of the time, Pallas kernels for 0%

profile of v1, /device:TPU:0, one launch (start us, length us, event | category | flops | bytes accessed | tf_op | source)
XLA Modules:
  0.0 751.9 jit_solution(4736391886292975710)
XLA Ops:
  19.2 7.5 all-to-all-start.2
  27.0 41.3 %all-reduce.1 = bf16[3584]{0:T(1024)(128)(2,1)S(1)} all-reduce(bf16[3584]{0:T(1024)(128)(2,1)S(1)} %dynamic-update-slice), channel_id=2, replica_groups=mesh['fsdp'=32] {'fsdp'}, use_global_device_ids=true, to_apply=%add.1 | all-reduce | flops 3584 | bytes 14336
  87.4 4.8 all-to-all-start.3
  94.5 23.5 %all-to-all-done.3 = bf16[32,2,1,4,1024]{4,3,1,2,0:T(4,128)(2,1)S(1)} async-done(((bf16[32,2,1,4,1024]{4,3,1,2,0:T(4,128)(2,1)}), bf16[32,2,1,4,1024]{4,3,1,2,0:T(4,128)(2,1)S(1)}, u32[]{:S(2)}, u32[]{:S(2)}) %all-to-all-start.3) | async-done | bytes 524320 | tf_op jit(solution)/shard_map/all_to_all | solution.py:134
  118.3 6.1 fusion.161
  124.4 138.7 %all-gather.4.cloned.1.call-done = bf16[1024,13824]{1,0:T(8,128)(2,1)} async-done(((bf16[32,13824]{1,0:T(8,128)(2,1)}), bf16[1024,13824]{1,0:T(8,128)(2,1)}) %all-gather.4.cloned.1.call-update) | async-done | bytes 28311568 | tf_op jit(solution)/shard_map/all_gather | solution.py:139
  314.2 4.7 fusion.4
  318.9 7.9 %fusion.19 = (bf16[256,2816]{1,0:T(8,128)(2,1)}, bf16[256,2816]{1,0:T(8,128)(2,1)}, bf16[256,2816]{1,0:T(8,128)(2,1)S(1)}) fusion(f32[256,2816]{1,0:T(8,128)S(1)} %copy-done.62, f32[256,2816]{1,0:T(8,128)S(1)} %fusion.4, bf16[256,1024]{1,0:T(8,128)(2,1)S(1)} %multiply_convert_fusion.5, bf16[1024,13824]{1,0:T(8,128)(2,1)} %all-gather.4.cloned.1.call-done), kind=kOutput, calls=%fused_computation.28 | convolution fusion | flops 1494417408 | bytes 16384000 | tf_op jit(solution)/shard_map/dot_general | solution.py:20
  327.9 4.2 convolution_convert_fusion
  332.2 4.9 fusion.2
  337.0 4.5 multiply_reduce_fusion.2
  350.0 4.2 multiply_reduce_fusion
  377.3 4.0 fusion.108
  402.1 4.2 copy.221
  408.6 4.0 copy.222
  422.6 4.0 copy.224
  429.3 4.0 copy.225
  460.3 4.2 convert_dynamic-update-slice_fusion.1
  464.5 4.2 convert_dynamic-update-slice_fusion
  474.8 7.6 %reshape.355 = f32[32,128,129]{2,1,0:T(8,128)} reshape(f32[32,16512]{1,0:T(8,128)} %pad_convert_fusion) | data formatting | bytes 4227072 | tf_op jit(solution)/shard_map/reshape | solution.py:73
  485.8 6.5 fusion.86
  530.5 4.5 fusion.54
  536.2 6.7 all-to-all-done.1
  546.0 194.9 %reduce-scatter.3.cloned.1.call-done = bf16[32,13824]{1,0:T(8,128)(2,1)} async-done(((bf16[1024,13824]{1,0:T(8,128)(2,1)}), bf16[32,13824]{1,0:T(8,128)(2,1)}) %reduce-scatter.3.cloned.1.call-update) | async-done | bytes 884752 | tf_op jit(solution)/shard_map/reduce_scatter | solution.py:149
  (314 shorter events, 235.4 us)
Async XLA Ops:
  7.2 279.0 %copy-start = (bf16[2,1,256,1024]{3,2,1,0:T(8,128)(2,1)S(1)}, bf16[2,1,256,1024]{3,2,1,0:T(8,128)(2,1)}, u32[]{:S(2)}) copy-start(bf16[2,1,256,1024]{3,2,1,0:T(8,128)(2,1)} %param.25) | copy-start | bytes 3145732
  7.2 10.4 %copy-start.51 = (bf16[2,1,128,1024]{3,2,1,0:T(8,128)(2,1)S(1)}, bf16[2,1,128,1024]{3,2,1,0:T(8,128)(2,1)}, u32[]{:S(2)}) copy-start(bf16[2,1,128,1024]{3,2,1,0:T(8,128)(2,1)} %param.26) | copy-start | bytes 1572868
  7.2 111.0 %all-gather.6.cloned.1.call-start = ((), (), s32[]{:S(2)}) async-start(), calls=%async_computation.8 | async-start | bytes 5947392 | tf_op jit(solution)/shard_map/all_gather | solution.py:144
  8.0 18.7 %copy-start.58 = (bf16[16]{0:T(256)(128)(2,1)S(1)}, bf16[16]{0:T(256)(128)(2,1)}, u32[]{:S(2)}) copy-start(bf16[16]{0:T(256)(128)(2,1)} %param.34) | copy-start | bytes 100
  8.0 18.7 %copy-start.59 = (bf16[32]{0:T(256)(128)(2,1)S(1)}, bf16[32]{0:T(256)(128)(2,1)}, u32[]{:S(2)}) copy-start(bf16[32]{0:T(256)(128)(2,1)} %param.33) | copy-start | bytes 196
  8.0 18.7 %copy-start.60 = (bf16[32]{0:T(256)(128)(2,1)S(1)}, bf16[32]{0:T(256)(128)(2,1)}, u32[]{:S(2)}) copy-start(bf16[32]{0:T(256)(128)(2,1)} %param.32) | copy-start | bytes 196
  8.0 18.7 %copy-start.61 = (bf16[32]{0:T(256)(128)(2,1)S(1)}, bf16[32]{0:T(256)(128)(2,1)}, u32[]{:S(2)}) copy-start(bf16[32]{0:T(256)(128)(2,1)} %param.31) | copy-start | bytes 196
  8.0 255.1 %all-gather.4.cloned.1.call-start = ((), (), s32[]{:S(2)}) async-start(), calls=%async_computation.7 | async-start | bytes 29196288 | tf_op jit(solution)/shard_map/all_gather | solution.py:139
  19.2 65.0 %all-to-all-start.2 = ((bf16[32,2,1,4,1024]{4,3,1,2,0:T(4,128)(2,1)}), bf16[32,2,1,4,1024]{4,3,1,2,0:T(4,128)(2,1)}, u32[]{:S(2)}, u32[]{:S(2)}) async-start(bf16[32,2,1,4,1024]{4,3,1,2,0:T(4,128)(2,1)} %copy.194), calls=%async_computation.2 | async-start | bytes 1048576 | tf_op jit(solution)/shard_map/all_to_all | solution.py:130
  81.3 11.9 %copy-start.27 = (bf16[2,1,128,1024]{3,2,1,0:T(8,128)(2,1)S(1)}, bf16[2,1,128,1024]{3,2,1,0:T(8,128)(2,1)}, u32[]{:S(2)}) copy-start(bf16[2,1,128,1024]{3,2,1,0:T(8,128)(2,1)} %param.24) | copy-start | bytes 1572868
  87.4 30.5 %all-to-all-start.3 = ((bf16[32,2,1,4,1024]{4,3,1,2,0:T(4,128)(2,1)}), bf16[32,2,1,4,1024]{4,3,1,2,0:T(4,128)(2,1)S(1)}, u32[]{:S(2)}, u32[]{:S(2)}) async-start(bf16[32,2,1,4,1024]{4,3,1,2,0:T(4,128)(2,1)} %fusion.131), calls=%async_computation.3 | async-start | bytes 1048576 | tf_op jit(solution)/shard_map/all_to_all | solution.py:134
  92.2 452.1 %reduce-scatter.5.cloned.1.call-start = ((), (), s32[]{:S(2)}) async-start(), calls=%async_computation.10 | async-start | bytes 5947392 | tf_op jit(solution)/shard_map/reduce_scatter | solution.py:154
  118.2 6.1 copy-start.36
  292.9 18.4 %copy-start.6 = (f32[256,1024]{1,0:T(8,128)}, f32[256,1024]{1,0:T(8,128)S(1)}, u32[]{:S(2)}) copy-start(f32[256,1024]{1,0:T(8,128)S(1)} %get-tuple-element.123) | copy-start | bytes 3145732
  314.0 27.6 %copy-start.14 = (f32[256,1024]{1,0:T(8,128)}, f32[256,1024]{1,0:T(8,128)S(1)}, u32[]{:S(2)}) copy-start(f32[256,1024]{1,0:T(8,128)S(1)} %get-tuple-element.127) | copy-start | bytes 3145732
  318.9 9.0 %copy-start.37 = (bf16[256,1024]{1,0:T(8,128)(2,1)S(1)}, bf16[256,1024]{1,0:T(8,128)(2,1)}, u32[]{:S(2)}) copy-start(bf16[256,1024]{1,0:T(8,128)(2,1)} %copy-done.36) | copy-start | bytes 1572868
  332.1 408.8 %reduce-scatter.3.cloned.1.call-start = ((), (), s32[]{:S(2)}) async-start(), calls=%async_computation.9 | async-start | bytes 29196288 | tf_op jit(solution)/shard_map/reduce_scatter | solution.py:149
  342.9 7.1 copy-start.48
  492.2 6.1 copy-start.55
  494.7 6.8 copy-start.35
  494.7 19.1 %all-to-all-start = ((bf16[32,2,1,4,1024]{4,3,1,2,0:T(4,128)(2,1)}), bf16[32,2,1,4,1024]{4,3,1,2,0:T(4,128)(2,1)}, u32[]{:S(2)}, u32[]{:S(2)}) async-start(bf16[32,2,1,4,1024]{4,3,1,2,0:T(4,128)(2,1)} %bitcast.239), calls=%async_computation | async-start | bytes 1048576 | tf_op jit(solution)/shard_map/all_to_all | solution.py:130
  511.4 15.9 %copy-start.44 = (bf16[128,8,2,256]{3,1,2,0:T(8,128)(2,1)S(1)}, bf16[128,8,2,256]{3,1,2,0:T(8,128)(2,1)}, u32[]{:S(2)}) copy-start(bf16[128,8,2,256]{3,1,2,0:T(8,128)(2,1)} %copy.253) | copy-start | bytes 3145732
  513.8 10.6 %all-to-all-start.4 = ((f32[32,1,112]{2,1,0:T(1,128)}), f32[32,1,112]{2,1,0:T(1,128)S(1)}, u32[]{:S(2)}, u32[]{:S(2)}) async-start(f32[32,1,112]{2,1,0:T(1,128)} %bitcast.46), calls=%async_computation.4 | async-start | bytes 32768 | tf_op jit(solution)/shard_map/all_to_all | solution.py:308
  524.4 18.5 %all-to-all-start.1 = ((bf16[32,2,1,4,1024]{4,3,1,2,0:T(4,128)(2,1)}), bf16[32,2,1,4,1024]{4,3,1,2,0:T(4,128)(2,1)S(1)}, u32[]{:S(2)}, u32[]{:S(2)}) async-start(bf16[32,2,1,4,1024]{4,3,1,2,0:T(4,128)(2,1)} %fusion.132), calls=%async_computation.1 | async-start | bytes 1048576 | tf_op jit(solution)/shard_map/all_to_all | solution.py:134
  (51 other events, 139.2 us)
Sparse Core Ops, SparseCore 0:
  10.9 72.8 all-gather.5
  87.2 175.8 all-gather.3
  332.2 143.4 reduce-scatter.4
  482.0 258.8 reduce-scatter.2
